TPU v7x, 32 devices: a whole 2x2x4 slice. The times are simulated.
32 devices in a mesh: freq: 4 (over y, x), panel: 8 (over z, core).
Axes of the slice: x: 2, y: 2, z: 4, core: 2. Of those that a mesh axis runs over, the one named last changes fastest.
Arguments:
- traces: bfloat16 [640, 640, 1024], P('panel', 'freq'), may hold values from -6 to 6
- filters: float32 [16, 7, 64], replicated, may hold values from -0.25 to 0.25
Outputs:
- primaries: bfloat16 [640, 640, 1024], P('panel', 'freq')
All inputs are finite; a program needn't handle non-finite values.
Results may differ from a plain program's by a relative error of at most 0.0095.
Values may be sent and summed in bfloat16 or wider, within the bound.
A program may use at most 192 MiB of HBM per device.

v0:
```python
import math
import jax
import jax.numpy as jnp
from jax import lax
from jax.sharding import PartitionSpec as P

NS = 640
NT = 1024
NF = 96
FLO = 8
TAPS = 64
SPAN = 7
RWIN = 40


def wave_table(freq_bins, sample_index):
    phases = freq_bins[:, None] * sample_index[None, :] % NT
    angles = phases.astype(jnp.float32) * jnp.float32(2.0 * math.pi / NT)
    return (jnp.cos(angles), jnp.sin(angles))


def complex_product(left_side, right_side):

    def factor_product(leading_factor, trailing_factor):
        return jnp.einsum(
            "gjo,god->gjd", leading_factor, trailing_factor, preferred_element_type=jnp.float32
        )

    part_real = factor_product(left_side[0], right_side[0]) - factor_product(
        left_side[1], right_side[1]
    )
    part_imag = factor_product(left_side[0], right_side[1]) + factor_product(
        left_side[1], right_side[0]
    )
    return jnp.stack([part_real, part_imag])


def response(filters, freq_bins):
    tap_index = jnp.arange(TAPS, dtype=jnp.int32)
    cosine_wave, sine_wave = wave_table(freq_bins, tap_index)
    filter_real = jnp.einsum("fk,wjk->fjw", cosine_wave, filters, precision=lax.Precision.HIGHEST)
    filter_imag = -jnp.einsum("fk,wjk->fjw", sine_wave, filters, precision=lax.Precision.HIGHEST)
    return (jnp.repeat(filter_real, RWIN, axis=2), jnp.repeat(filter_imag, RWIN, axis=2))


def apply_filter(extended, filter_real, filter_imag, source_count):
    sum_real = jnp.zeros(extended.shape[1:2] + (source_count,) + extended.shape[3:], jnp.float32)
    sum_imag = jnp.zeros_like(sum_real)
    for shifted in range(SPAN):
        part_real = extended[0, :, shifted : shifted + source_count, :]
        part_imag = extended[1, :, shifted : shifted + source_count, :]
        weight_real = filter_real[:, shifted][:, None, :]
        weight_imaginary = filter_imag[:, shifted][:, None, :]
        sum_real = sum_real + weight_real * part_real - weight_imaginary * part_imag
        sum_imag = sum_imag + weight_real * part_imag + weight_imaginary * part_real
    return jnp.stack([sum_real, sum_imag])


def per_device(traces, filters):
    shot_rows, receiver_cols, time_sample_count = traces.shape
    rim_width = SPAN // 2
    scale_sources = jnp.float32(math.sqrt(NS))
    freq_bins = FLO + jnp.arange(NF, dtype=jnp.int32)
    cosine_wave, sine_wave = wave_table(freq_bins, jnp.arange(NT, dtype=jnp.int32))
    forward = (jnp.concatenate([cosine_wave, -sine_wave], 0) / jnp.float32(math.sqrt(NT))).astype(
        jnp.bfloat16
    )
    reciprocal_value = jnp.concatenate([cosine_wave, -sine_wave], 0).astype(jnp.bfloat16)
    spectra = jnp.einsum("srt,ct->csr", traces, forward, preferred_element_type=jnp.float32)
    spectra = spectra.astype(jnp.bfloat16).reshape(2, NF, shot_rows, receiver_cols)
    columns = lax.all_to_all(spectra, "panel", split_axis=1, concat_axis=2, tiled=True)
    slice_count = columns.shape[1]
    first_slice = lax.axis_index("panel") * slice_count
    complete = lax.all_gather(columns, "freq", axis=3, tiled=True)
    order_one = (complex_product(complete, columns) / scale_sources).astype(jnp.bfloat16)
    order_two = complex_product(complete, order_one) / scale_sources
    prediction = (order_one.astype(jnp.float32) - order_two).astype(jnp.bfloat16)
    extended = jnp.pad(
        prediction.astype(jnp.float32), ((0, 0), (0, 0), (rim_width, rim_width), (0, 0))
    )
    own_bins = FLO + first_slice + jnp.arange(slice_count, dtype=jnp.int32)
    filter_real, filter_imag = response(filters, own_bins)
    receiver_start = lax.axis_index("freq") * receiver_cols
    filter_real = lax.dynamic_slice_in_dim(filter_real, receiver_start, receiver_cols, 2)
    filter_imag = lax.dynamic_slice_in_dim(filter_imag, receiver_start, receiver_cols, 2)
    matched = apply_filter(extended, filter_real, filter_imag, NS)
    returned = lax.all_to_all(
        matched.astype(jnp.bfloat16), "panel", split_axis=2, concat_axis=1, tiled=True
    )
    matched_rows = returned.reshape(2 * NF, shot_rows, receiver_cols)
    multiples = jnp.einsum(
        "csr,ct->srt", matched_rows, reciprocal_value, preferred_element_type=jnp.float32
    )
    multiples = multiples / jnp.float32(math.sqrt(NF))
    return (traces.astype(jnp.float32) - multiples).astype(jnp.bfloat16)


def solution(mesh):
    placed = (P("panel", "freq", None), P())
    return jax.shard_map(
        per_device, mesh=mesh, in_specs=placed, out_specs=P("panel", "freq", None), check_vma=False
    )
```

profile of v0, /device:TPU:0, one launch (start us, length us, event | category | flops | bytes accessed | tf_op | source)
XLA Modules:
  0.0 942.0 jit_solution(9572457835950158956)
XLA Ops:
  9.1 13.8 %convolution_convert_fusion = bf16[192,80,160]{0,2,1:T(8,128)(2,1)} fusion(bf16[80,160,1024]{2,1,0:T(8,128)(2,1)} %param.2, f32[96,1024]{1,0:T(8,128)S(1)} %get-tuple-element.24, f32[96,1024]{1,0:T(8,128)S(1)} %get-tuple-element.23), kind=kOutput, calls=%fused_computation.35 | convolution fusion | flops 5036212224 | bytes 31916032 | tf_op jit(solution)/shard_map/srt,ct->csr/dot_general | solution.py:69
  22.9 15.0 %reshape.26 = bf16[2,96,80,160]{1,0,3,2:T(2,128)(2,1)} reshape(bf16[192,80,160]{0,2,1:T(8,128)(2,1)} %convolution_convert_fusion) | data formatting | bytes 9830400 | tf_op jit(solution)/shard_map/reshape | solution.py:70
  37.9 17.3 %copy.39 = bf16[2,96,80,160]{3,2,0,1:T(8,128)(2,1)} copy(bf16[2,96,80,160]{1,0,3,2:T(2,128)(2,1)} %reshape.26) | data formatting | bytes 9830400 | tf_op jit(solution)/shard_map/reshape | solution.py:70
  55.2 179.6 %all_to_all.33 = bf16[2,96,80,160]{3,2,0,1:T(8,128)(2,1)} all-to-all(bf16[2,96,80,160]{3,2,0,1:T(8,128)(2,1)} %copy.39), channel_id=1, replica_groups=mesh['freq'=4,'panel'=8] {'panel'}, dimensions={1} | all-to-all | bytes 9830400 | tf_op jit(solution)/shard_map/all_to_all | solution.py:71
  234.8 12.6 %copy.52 = bf16[2,12,8,80,160]{3,2,0,1,4:T(8,128)(2,1)} copy(bf16[2,12,8,80,160]{4,3,0,1,2:T(8,128)(2,1)} %bitcast.133) | data formatting | bytes 9830400 | tf_op jit(solution)/shard_map/all_to_all | solution.py:71
  247.4 16.3 %reshape.33 = bf16[2,12,640,160]{2,0,1,3:T(2,128)(2,1)} reshape(bf16[2,12,8,80,160]{3,2,0,1,4:T(8,128)(2,1)} %copy.52) | data formatting | bytes 9830400 | tf_op jit(solution)/shard_map/all_to_all | solution.py:71
  267.5 4.5 copy.40
  272.0 4.5 fusion.67
  276.5 6.7 copy.46
  283.2 5.5 squeeze.15
  288.7 6.4 copy.44
  295.1 6.6 squeeze.13
  301.7 144.0 %all-gather.2.cloned.1.call-done = bf16[2,12,640,640]{2,0,1,3:T(2,128)(2,1)} async-done(((bf16[2,12,640,160]{2,0,1,3:T(2,128)(2,1)}), bf16[2,12,640,640]{2,0,1,3:T(2,128)(2,1)}) %all-gather.2.cloned.1.call-update) | async-done | bytes 19660816 | tf_op jit(solution)/shard_map/all_gather | solution.py:74
  445.7 38.6 %fusion.66 = (bf16[1,12,640,640]{2,0,1,3:T(2,128)(2,1)}, bf16[1,12,640,640]{2,0,1,3:T(2,128)(2,1)}) fusion(bf16[2,12,640,640]{2,0,1,3:T(2,128)(2,1)} %all-gather.2.cloned.1.call-done), kind=kLoop, calls=%fused_computation.120 | loop fusion | bytes 39321600 | tf_op jit(solution)/shard_map/slice | solution.py:29
  484.4 38.2 %copy.68 = bf16[1,12,640,640]{3,2,1,0:T(8,128)(2,1)} copy(bf16[1,12,640,640]{2,0,1,3:T(2,128)(2,1)} %get-tuple-element.5) | data formatting | bytes 19660800
  522.6 38.4 %copy.69 = bf16[1,12,640,640]{3,2,1,0:T(8,128)(2,1)} copy(bf16[1,12,640,640]{2,0,1,3:T(2,128)(2,1)} %get-tuple-element.6) | data formatting | bytes 19660800
  561.0 10.0 %fusion.7 = f32[12,640,160]{1,2,0:T(8,128)} fusion(bf16[12,640,160]{1,2,0:T(8,128)(2,1)} %squeeze.13, bf16[1,12,640,640]{3,2,1,0:T(8,128)(2,1)} %copy.69), kind=kOutput, calls=%fused_computation.22 | convolution fusion | flops 1572864000 | bytes 17203200 | tf_op jit(solution)/shard_map/gjo,god->gjd/dot_general | solution.py:25
  571.0 9.3 fusion.9
  580.3 10.8 %add_bitcast_fusion.1 = f32[1,12,640,160]{2,3,1,0:T(8,128)} fusion(f32[12,640,160]{1,2,0:T(8,128)} %fusion.7, bf16[12,640,160]{1,2,0:T(8,128)(2,1)S(1)} %squeeze.15, bf16[1,12,640,640]{3,2,1,0:T(8,128)(2,1)} %copy.68), kind=kOutput, calls=%fused_computation.42 | convolution fusion | flops 1574092800 | bytes 22118400 | tf_op jit(solution)/shard_map/gjo,god->gjd/dot_general | solution.py:25
  591.1 11.4 %subtract_bitcast_fusion.1 = f32[1,12,640,160]{2,3,1,0:T(8,128)} fusion(f32[12,640,160]{1,2,0:T(8,128)} %fusion.9, bf16[12,640,160]{1,2,0:T(8,128)(2,1)} %squeeze.13, bf16[1,12,640,640]{3,2,1,0:T(8,128)(2,1)} %copy.68), kind=kOutput, calls=%fused_computation.43 | convolution fusion | flops 1574092800 | bytes 22118400 | tf_op jit(solution)/shard_map/gjo,god->gjd/dot_general | solution.py:25
  602.6 5.1 fusion
  607.6 11.4 %fusion.3 = f32[12,640,160]{1,2,0:T(8,128)} fusion(bf16[1,12,640,640]{3,2,1,0:T(8,128)(2,1)} %copy.69, bf16[2,12,640,160]{2,3,1,0:T(8,128)(2,1)S(1)} %fusion), kind=kOutput, calls=%fused_computation.18 | convolution fusion | flops 1572864000 | bytes 17203200 | tf_op jit(solution)/shard_map/gjo,god->gjd/dot_general | solution.py:25
  619.0 9.3 fusion.5
  628.4 11.5 %subtract_bitcast_fusion = f32[1,12,640,160]{2,3,1,0:T(8,128)} fusion(f32[12,640,160]{1,2,0:T(8,128)} %fusion.5, bf16[1,12,640,640]{3,2,1,0:T(8,128)(2,1)} %copy.68, bf16[2,12,640,160]{2,3,1,0:T(8,128)(2,1)} %copy-done.2), kind=kOutput, calls=%fused_computation.41 | convolution fusion | flops 1574092800 | bytes 22118400 | tf_op jit(solution)/shard_map/gjo,god->gjd/dot_general | solution.py:25
  639.8 11.5 %add_bitcast_fusion = f32[1,12,640,160]{2,3,1,0:T(8,128)} fusion(f32[12,640,160]{1,2,0:T(8,128)} %fusion.3, bf16[1,12,640,640]{3,2,1,0:T(8,128)(2,1)} %copy.68, bf16[2,12,640,160]{2,3,1,0:T(8,128)(2,1)} %copy-done.2), kind=kOutput, calls=%fused_computation.40 | convolution fusion | flops 1574092800 | bytes 22118400 | tf_op jit(solution)/shard_map/gjo,god->gjd/dot_general | solution.py:25
  651.3 7.4 fusion.20
  658.8 21.9 %add_convert_fusion = bf16[1,12,640,160]{2,3,1,0:T(8,128)(2,1)S(1)} fusion(f32[2,12,640,160]{2,3,1,0:T(8,128)S(1)} %fusion.20, f32[12,160]{1,0:T(8,128)S(1)} %bitcast.149, f32[12,160]{1,0:T(8,128)S(1)} %bitcast.151, f32[12,160]{1,0:T(8,128)S(1)} %bitcast.139, f32[12,160]{1,0:T(8,128)S(1)} %bitcast.161, f32[12,160]{1,0:T(8,128)S(1)} %bitcast.141, ...), kind=kLoop, calls=%fused_computation.38 | loop fusion | flops 34406400 | bytes 22347776 | tf_op jit(solution)/shard_map/convert.1
  680.6 21.9 %subtract_convert_fusion.1 = bf16[1,12,640,160]{2,3,1,0:T(8,128)(2,1)S(1)} fusion(f32[2,12,640,160]{2,3,1,0:T(8,128)S(1)} %fusion.20, f32[12,160]{1,0:T(8,128)S(1)} %bitcast.150, f32[12,160]{1,0:T(8,128)S(1)} %bitcast.152, f32[12,160]{1,0:T(8,128)S(1)} %bitcast.140, f32[12,160]{1,0:T(8,128)S(1)} %bitcast.162, f32[12,160]{1,0:T(8,128)S(1)} %bitcast.142, ...), kind=kLoop, calls=%fused_computation.39 | loop fusion | flops 34406400 | bytes 22347776 | tf_op jit(solution)/shard_map/convert
  705.3 19.4 %copy.48 = bf16[2,12,640,160]{3,0,1,2:T(2,128)(2,1)} copy(bf16[2,12,640,160]{2,3,1,0:T(8,128)(2,1)} %pad_maximum_fusion) | data formatting | bytes 9830400 | tf_op jit(solution)/shard_map/stack | solution.py:56
  724.7 177.2 %all_to_all.34 = bf16[2,12,640,160]{3,0,1,2:T(2,128)(2,1)S(1)} all-to-all(bf16[2,12,640,160]{3,0,1,2:T(2,128)(2,1)} %copy.48), channel_id=1, replica_groups=mesh['freq'=4,'panel'=8] {'panel'}, dimensions={2} | all-to-all | bytes 9830400 | tf_op jit(solution)/shard_map/all_to_all | solution.py:87
  902.0 4.9 copy.49
  906.9 27.9 %subtract_convert_fusion = bf16[80,160,1024]{2,1,0:T(8,128)(2,1)} fusion(bf16[80,160,1024]{2,1,0:T(8,128)(2,1)} %param.2, bf16[192,80,160]{2,1,0:T(8,128)(2,1)} %bitcast.136, f32[96,1024]{1,0:T(8,128)S(1)} %copy-done.6, f32[96,1024]{1,0:T(8,128)S(1)} %copy-done.4), kind=kOutput, calls=%fused_computation | convolution fusion | flops 5086380032 | bytes 58130432 | tf_op jit(solution)/shard_map/csr,ct->srt/dot_general | solution.py:91
  (45 shorter events, 8.8 us)
Async XLA Ops:
  6.5 257.3 %copy-start = (f32[16,7,64]{2,0,1:T(8,128)S(1)}, f32[16,7,64]{2,0,1:T(8,128)}, u32[]{:S(2)}) copy-start(f32[16,7,64]{2,0,1:T(8,128)} %param.3) | copy-start | bytes 86020
  6.5 439.2 %all-gather.2.cloned.1.call-start = ((), (), s32[]{:S(2)}) async-start(), calls=%async_computation.2 | async-start | bytes 24576000 | tf_op jit(solution)/shard_map/all_gather | solution.py:74
  8.2 0.7 copy-start.3
  8.2 0.9 copy-start.5
  607.6 11.4 %copy-start.2 = (bf16[2,12,640,160]{2,3,1,0:T(8,128)(2,1)}, bf16[2,12,640,160]{2,3,1,0:T(8,128)(2,1)S(1)}, u32[]{:S(2)}) copy-start(bf16[2,12,640,160]{2,3,1,0:T(8,128)(2,1)S(1)} %fusion) | copy-start | bytes 14745604
  651.3 7.4 copy-start.7
  901.9 4.9 copy-start.4
  902.0 4.9 copy-start.6
  906.9 27.9 %copy-start.1 = (f32[16,7,64]{2,0,1:T(8,128)S(1)}, f32[16,7,64]{2,0,1:T(8,128)}, u32[]{:S(2)}) copy-start(f32[16,7,64]{2,0,1:T(8,128)} %param.3) | copy-start | bytes 86020
Sparse Core Ops, SparseCore 0:
  263.9 181.7 all-gather.1
where the time goes:
time: 952 us; the launch traced here: 942 us
  blocking collectives  357 us (38%)
  local copies, waits for them, and re-layouts  238 us (25%)
  waiting for transfers between devices  144 us (15%)
  matrix products  128 us (13%)
  other arithmetic  60.6 us (6%)
  between operations  14.1 us (1%)
    all_to_all x1, blocking collectives, per_device(): lax.all_to_all(spectra, 'panel', split_axis=1, concat_axis=2, tiled=True)  180 us
    all_to_all x1, blocking collectives, per_device(): lax.all_to_all(matched.astype(jnp.bfloat16), 'panel', split_axis=2, conca...  177 us
    all_gather x1, waiting for transfers between devices, per_device(): complete = lax.all_gather(columns, 'freq', axis=3, tiled=True)  144 us
    dot_general x8, matrix products, factor_product(): jnp.einsum('gjo,god->gjd', leading_factor, trailing_factor, preferred_ele...  85.3 us
    unnamed x32, local copies, waits for them, and re-layouts  78.2 us
    another operation x2, other arithmetic  43.8 us
    slice x1, local copies, waits for them, and re-layouts, complex_product(): left_side[0]  38.6 us
    all_to_all x3, local copies, waits for them, and re-layouts, per_device(): lax.all_to_all(spectra, 'panel', split_axis=1, concat_axis=2, tiled=True)  33.4 us
  transfers between devices with their start and end apart: 1, of which 1 were waited for; matrix products, arithmetic and copies ran while one was open for 4% of the time, Pallas kernels for 0%

commit v1 on v0

--- a/solution.py
+++ b/solution.py
@@ -71,7 +71,7 @@
     columns = lax.all_to_all(spectra, "panel", split_axis=1, concat_axis=2, tiled=True)
     slice_count = columns.shape[1]
     first_slice = lax.axis_index("panel") * slice_count
-    complete = lax.all_gather(columns, "freq", axis=3, tiled=True)
+    complete = jnp.concatenate(lax.all_gather(columns, "freq"), axis=3)
     order_one = (complex_product(complete, columns) / scale_sources).astype(jnp.bfloat16)
     order_two = complex_product(complete, order_one) / scale_sources
     prediction = (order_one.astype(jnp.float32) - order_two).astype(jnp.bfloat16)

time: 952 us -> 817 us (0.86)
  local copies, waits for them, and re-layouts: 238 us -> 144 us
  matrix products: 128 us -> 87.9 us
    unnamed x32 -> x28, local copies, waits for them, and re-layouts: 78.2 us -> 2.31 us
    dot_general x8, matrix products: 85.3 us -> 45.1 us  [factor_product(): jnp.einsum('gjo,god->gjd', leading_factor, trailing_factor, preferred_ele...]
    slice x1, local copies, waits for them, and re-layouts: 38.6 us -> 8.21 us  [complex_product(): left_side[0]]
    all_gather x0 -> x2, local copies, waits for them, and re-layouts: none -> 29.2 us  [per_device(): complete = jnp.concatenate(lax.all_gather(columns, 'freq'), axis=3)]
    all_to_all x3 -> x2, local copies, waits for them, and re-layouts: 33.4 us -> 15.7 us  [per_device(): lax.all_to_all(spectra, 'panel', split_axis=1, concat_axis=2, tiled=True)]
  transfers between devices with their start and end apart: 1 -> 1, of which waited for: 1 -> 1; matrix products, arithmetic and copies ran while one was open for 4% -> 5% of each run, Pallas kernels for 0% -> 0%
where the time goes in v1:
time: 817 us; the launch traced here: 808 us
  blocking collectives  357 us (44%)
  local copies, waits for them, and re-layouts  144 us (18%)
  waiting for transfers between devices  144 us (18%)
  matrix products  87.9 us (11%)
  other arithmetic  60.4 us (7%)
  between operations  14.1 us (2%)
    all_to_all x1, blocking collectives, per_device(): lax.all_to_all(spectra, 'panel', split_axis=1, concat_axis=2, tiled=True)  180 us
    all_to_all x1, blocking collectives, per_device(): lax.all_to_all(matched.astype(jnp.bfloat16), 'panel', split_axis=2, conca...  178 us
    all_gather x1, waiting for transfers between devices, per_device(): complete = jnp.concatenate(lax.all_gather(columns, 'freq'), axis=3)  144 us
    dot_general x8, matrix products, factor_product(): jnp.einsum('gjo,god->gjd', leading_factor, trailing_factor, preferred_ele...  45.1 us
    another operation x2, other arithmetic  43.6 us
    reshape x2, local copies, waits for them, and re-layouts, per_device(): spectra.astype(jnp.bfloat16).reshape(2, NF, shot_rows, receiver_cols)  32.3 us
    all_gather x2, local copies, waits for them, and re-layouts, per_device(): complete = jnp.concatenate(lax.all_gather(columns, 'freq'), axis=3)  29.2 us
    dot_general x1, matrix products, per_device(): jnp.einsum('csr,ct->srt', matched_rows, reciprocal_value, preferred_eleme...  27.9 us
  transfers between devices with their start and end apart: 1, of which 1 were waited for; matrix products, arithmetic and copies ran while one was open for 5% of the time, Pallas kernels for 0%

profile of v1, /device:TPU:0, one launch (start us, length us, event | category | flops | bytes accessed | tf_op | source)
XLA Modules:
  0.0 808.3 jit_solution(12509804548485124335)
XLA Ops:
  9.1 13.8 %convolution_convert_fusion = bf16[192,80,160]{0,2,1:T(8,128)(2,1)} fusion(bf16[80,160,1024]{2,1,0:T(8,128)(2,1)} %param.2, f32[96,1024]{1,0:T(8,128)S(1)} %get-tuple-element.24, f32[96,1024]{1,0:T(8,128)S(1)} %get-tuple-element.23), kind=kOutput, calls=%fused_computation.20 | convolution fusion | flops 5036212224 | bytes 31916032 | tf_op jit(solution)/shard_map/srt,ct->csr/dot_general | solution.py:69
  22.8 15.0 %reshape.35 = bf16[2,96,80,160]{1,0,3,2:T(2,128)(2,1)} reshape(bf16[192,80,160]{0,2,1:T(8,128)(2,1)} %convolution_convert_fusion) | data formatting | bytes 9830400 | tf_op jit(solution)/shard_map/reshape | solution.py:70
  37.8 17.3 %copy.59 = bf16[2,96,80,160]{3,2,0,1:T(8,128)(2,1)} copy(bf16[2,96,80,160]{1,0,3,2:T(2,128)(2,1)} %reshape.35) | data formatting | bytes 9830400 | tf_op jit(solution)/shard_map/reshape | solution.py:70
  55.2 179.6 %all_to_all.30 = bf16[2,96,80,160]{3,2,0,1:T(8,128)(2,1)} all-to-all(bf16[2,96,80,160]{3,2,0,1:T(8,128)(2,1)} %copy.59), channel_id=1, replica_groups=mesh['freq'=4,'panel'=8] {'panel'}, dimensions={1} | all-to-all | bytes 9830400 | tf_op jit(solution)/shard_map/all_to_all | solution.py:71
  234.8 11.6 %copy.61 = bf16[2,12,8,80,160]{3,2,4,1,0:T(8,128)(2,1)} copy(bf16[2,12,8,80,160]{4,3,0,1,2:T(8,128)(2,1)} %bitcast.133) | data formatting | bytes 9830400 | tf_op jit(solution)/shard_map/all_to_all | solution.py:71
  246.5 12.1 %all_gather.6 = bf16[1,2,12,640,160]{3,4,2,1,0:T(8,128)(2,1)} reshape(bf16[2,12,8,80,160]{3,2,4,1,0:T(8,128)(2,1)} %copy.61) | data formatting | bytes 9830400 | tf_op jit(solution)/shard_map/all_gather | solution.py:74
  261.8 4.0 copy.60
  265.8 4.8 fusion.47
  270.6 6.9 copy.63
  277.6 5.5 squeeze.13
  283.1 6.4 copy.65
  289.5 6.6 squeeze.15
  296.1 144.4 %all-gather.2.cloned.1.call-done = bf16[4,2,12,640,160]{3,4,2,1,0:T(8,128)(2,1)} async-done(((bf16[1,2,12,640,160]{3,4,2,1,0:T(8,128)(2,1)}), bf16[4,2,12,640,160]{3,4,2,1,0:T(8,128)(2,1)}) %all-gather.2.cloned.1.call-update) | async-done | bytes 19660816 | tf_op jit(solution)/shard_map/all_gather | solution.py:74
  440.6 17.0 %copy.117 = bf16[4,2,12,640,160]{3,4,0,2,1:T(8,128)(2,1)} copy(bf16[4,2,12,640,160]{3,4,2,1,0:T(8,128)(2,1)} %all-gather.2.cloned.1.call-done) | data formatting | bytes 39321600 | tf_op jit(solution)/shard_map/all_gather | solution.py:74
  457.6 8.2 %fusion.46 = (bf16[1,12,640,4,160]{2,4,3,1,0:T(8,128)(2,1)S(1)}, bf16[1,12,640,4,160]{2,4,3,1,0:T(8,128)(2,1)S(1)}) fusion(bf16[2,12,640,4,160]{2,4,3,1,0:T(8,128)(2,1)} %bitcast.132), kind=kLoop, calls=%fused_computation.109 | loop fusion | bytes 39321600 | tf_op jit(solution)/shard_map/slice | solution.py:29
  465.8 2.5 fusion.48
  469.7 4.1 fusion.49
  473.8 6.5 subtract_bitcast_fusion.1
  480.3 4.9 add_bitcast_fusion.1
  485.2 5.1 fusion
  490.2 8.7 %fusion.5 = f32[12,640,160]{1,2,0:T(8,128)} fusion(bf16[12,640,640]{1,2,0:T(8,128)(2,1)} %bitcast.130, bf16[2,12,640,160]{2,3,1,0:T(8,128)(2,1)S(1)} %fusion), kind=kOutput, calls=%fused_computation.31 | convolution fusion | flops 1572864000 | bytes 17203200 | tf_op jit(solution)/shard_map/gjo,god->gjd/dot_general | solution.py:25
  499.0 2.5 fusion.6
  501.4 7.2 subtract_bitcast_fusion
  508.6 8.7 %add_bitcast_fusion = f32[1,12,640,160]{2,3,1,0:T(8,128)} fusion(f32[12,640,160]{1,2,0:T(8,128)S(1)} %fusion.6, bf16[12,640,640]{1,2,0:T(8,128)(2,1)} %bitcast.131, bf16[2,12,640,160]{2,3,1,0:T(8,128)(2,1)S(1)} %fusion), kind=kOutput, calls=%fused_computation.25 | convolution fusion | flops 1574092800 | bytes 22118400 | tf_op jit(solution)/shard_map/gjo,god->gjd/dot_general | solution.py:25
  517.3 7.4 fusion.4
  524.7 21.7 %subtract_convert_fusion.1 = bf16[1,12,640,160]{2,3,1,0:T(8,128)(2,1)S(1)} fusion(f32[2,12,640,160]{2,3,1,0:T(8,128)S(1)} %fusion.4, f32[12,160]{1,0:T(8,128)S(1)} %bitcast.137, f32[12,160]{1,0:T(8,128)S(1)} %bitcast.139, f32[12,160]{1,0:T(8,128)S(1)} %bitcast.141, f32[12,160]{1,0:T(8,128)S(1)} %bitcast.143, f32[12,160]{1,0:T(8,128)S(1)} %bitcast.145, ...), kind=kLoop, calls=%fused_computation.24 | loop fusion | flops 34406400 | bytes 22347776 | tf_op jit(solution)/shard_map/convert
  546.4 21.9 %add_convert_fusion = bf16[1,12,640,160]{2,3,1,0:T(8,128)(2,1)S(1)} fusion(f32[2,12,640,160]{2,3,1,0:T(8,128)S(1)} %fusion.4, f32[12,160]{1,0:T(8,128)S(1)} %bitcast.138, f32[12,160]{1,0:T(8,128)S(1)} %bitcast.140, f32[12,160]{1,0:T(8,128)S(1)} %bitcast.142, f32[12,160]{1,0:T(8,128)S(1)} %bitcast.144, f32[12,160]{1,0:T(8,128)S(1)} %bitcast.146, ...), kind=kLoop, calls=%fused_computation.23 | loop fusion | flops 34406400 | bytes 22347776 | tf_op jit(solution)/shard_map/convert.1
  568.3 2.7 pad_maximum_fusion
  571.0 19.4 %copy.74 = bf16[2,12,640,160]{3,0,1,2:T(2,128)(2,1)} copy(bf16[2,12,640,160]{2,3,1,0:T(8,128)(2,1)} %pad_maximum_fusion) | data formatting | bytes 9830400 | tf_op jit(solution)/shard_map/stack | solution.py:56
  590.5 177.8 %all_to_all.31 = bf16[2,12,640,160]{3,0,1,2:T(2,128)(2,1)S(1)} all-to-all(bf16[2,12,640,160]{3,0,1,2:T(2,128)(2,1)} %copy.74), channel_id=1, replica_groups=mesh['freq'=4,'panel'=8] {'panel'}, dimensions={2} | all-to-all | bytes 9830400 | tf_op jit(solution)/shard_map/all_to_all | solution.py:87
  768.2 4.9 copy.75
  773.1 27.9 %subtract_convert_fusion = bf16[80,160,1024]{2,1,0:T(8,128)(2,1)} fusion(bf16[80,160,1024]{2,1,0:T(8,128)(2,1)} %param.2, bf16[192,80,160]{2,1,0:T(8,128)(2,1)} %bitcast.136, f32[96,1024]{1,0:T(8,128)S(1)} %copy-done.6, f32[96,1024]{1,0:T(8,128)S(1)} %copy-done.4), kind=kOutput, calls=%fused_computation | convolution fusion | flops 5086380032 | bytes 58130432 | tf_op jit(solution)/shard_map/csr,ct->srt/dot_general | solution.py:91
  (42 shorter events, 6.9 us)
Async XLA Ops:
  6.5 252.1 %copy-start = (f32[16,7,64]{2,0,1:T(8,128)S(1)}, f32[16,7,64]{2,0,1:T(8,128)}, u32[]{:S(2)}) copy-start(f32[16,7,64]{2,0,1:T(8,128)} %param.3) | copy-start | bytes 86020
  6.5 434.0 %all-gather.2.cloned.1.call-start = ((), (), s32[]{:S(2)}) async-start(), calls=%async_computation.2 | async-start | bytes 24576000 | tf_op jit(solution)/shard_map/all_gather | solution.py:74
  8.2 0.7 copy-start.3
  8.2 0.9 copy-start.5
  465.8 3.9 copy-start.2
  768.2 4.9 copy-start.4
  768.2 4.9 copy-start.6
  773.1 27.9 %copy-start.1 = (f32[16,7,64]{2,0,1:T(8,128)S(1)}, f32[16,7,64]{2,0,1:T(8,128)}, u32[]{:S(2)}) copy-start(f32[16,7,64]{2,0,1:T(8,128)} %param.3) | copy-start | bytes 86020
Sparse Core Ops, SparseCore 0:
  258.7 181.7 all-gather.1
